TPU v7x, 256 devices: a whole 4x4x8 slice. The times are simulated.
256 devices in a mesh: blk: 32 (over x_lo, z, core), tp: 8 (over x_hi, y).
Axes of the slice: x: 4 (x_hi: 2, x_lo: 2; x = x_hi * 2 + x_lo), y: 4, z: 8, core: 2. Of those that a mesh axis runs over, the one named last changes fastest.
Arguments:
- tokens: bfloat16 [8192, 8192], P('blk', 'tp'), may hold values from -6 to 6
- weight: bfloat16 [8192, 2048], P('tp'), may hold values from -0.0625 to 0.0625
- bank_a: bfloat16 [32, 8192, 32], P('blk', 'tp'), may hold values from -0.0625 to 0.0625
- bank_b: bfloat16 [32, 32, 1024], P('blk'), may hold values from -1.5 to 1.5
- tile_map: int32 [64, 1], P('blk'), may hold values from 0 to 31
- grad_out: bfloat16 [8192, 2048], P(('blk', 'tp')), may hold values from -6 to 6
Outputs:
- key_value_output: bfloat16 [8192, 2048], P(('blk', 'tp'))
- token_gradient: bfloat16 [8192, 8192], P('blk', 'tp')
- grad_a: float32 [32, 8192, 32], P('blk', 'tp')
- grad_b: float32 [32, 32, 1024], P('blk', None, 'tp')
Inputs may be any that keep to these rules, and one draw needn't show every extreme that they name: `tile_map`: every one of the 32 adapters is the adapter of at least one tile.
All inputs are finite; a program needn't handle non-finite values.
Results may differ from a plain program's by a relative error of at most 0.003.
Values may be sent and summed in bfloat16 or wider, within the bound.
A program may use at most 64 MiB of HBM per device.

v0:
```python
import jax
import jax.numpy as jnp
from jax import lax
from jax.sharding import PartitionSpec as P

adapter_scale = 0.5


def on_device(tokens, weight, bank_a, bank_b, tile_map, grad_out):
    tile_index_list = tile_map[:, 0]
    grouped_row_count = tokens.shape[0]
    feature_shard = tokens.shape[1]
    tile_count = tile_index_list.shape[0]
    tile_rows = grouped_row_count // tile_count
    rank_two = bank_a.shape[2]
    rank_one = rank_two // 2
    kv_width = bank_b.shape[2]
    tp_count = lax.axis_size("tp")
    local_row_block = grouped_row_count // tp_count
    kv_dev = kv_width // tp_count
    adapt_local = bank_a.shape[0]
    empty = (
        jnp.zeros((tile_count, feature_shard, rank_two), jnp.bfloat16),
        jnp.zeros((tile_count, rank_two, kv_width), jnp.bfloat16),
    )
    whole_a, whole_b = (
        lax.all_gather(bank_a, "blk", axis=0, tiled=True),
        lax.all_gather(bank_b, "blk", axis=0, tiled=True),
    )
    pieces = (whole_a, whole_b)
    piece_rows = pieces[0].shape[0]
    one_hot = (tile_index_list[:, None] == jnp.arange(piece_rows, dtype=jnp.int32)[None, :]).astype(
        jnp.bfloat16
    )
    picked_a = jnp.dot(
        one_hot, pieces[0].reshape(piece_rows, -1), preferred_element_type=jnp.float32
    )
    picked_b = jnp.dot(
        one_hot, pieces[1].reshape(piece_rows, -1), preferred_element_type=jnp.float32
    )
    factor_down = picked_a.reshape(empty[0].shape).astype(jnp.bfloat16)
    fac_b = picked_b.reshape(empty[1].shape).astype(jnp.bfloat16)
    token_tile_index = tokens.reshape(tile_count, tile_rows, feature_shard)
    rank_part = jnp.einsum(
        "tre,tek->trk", token_tile_index, factor_down, preferred_element_type=jnp.float32
    )
    rank_act = lax.psum(rank_part, "tp").astype(jnp.bfloat16)
    base_local_rows = lax.psum_scatter(
        jnp.dot(tokens, weight, preferred_element_type=jnp.float32),
        "tp",
        scatter_dimension=0,
        tiled=True,
    )
    adapter_complete = jnp.concatenate(
        [
            jnp.einsum(
                "trk,tkc->trc",
                rank_act[:, :, :rank_one],
                fac_b[:, :rank_one],
                preferred_element_type=jnp.float32,
            ),
            jnp.einsum(
                "trk,tkc->trc",
                rank_act[:, :, rank_one:],
                fac_b[:, rank_one:],
                preferred_element_type=jnp.float32,
            ),
        ],
        axis=2,
    ).reshape(grouped_row_count, 2 * kv_width)
    first_row_index = lax.axis_index("tp") * local_row_block
    adapter_local_rows = lax.dynamic_slice_in_dim(
        adapter_complete, first_row_index, local_row_block, 0
    )
    key_value_output = (base_local_rows + adapter_scale * adapter_local_rows).astype(jnp.bfloat16)
    grad_rows = lax.all_gather(grad_out, "tp", axis=0, tiled=True)
    gradient_per_tile = grad_rows.reshape(tile_count, tile_rows, 2 * kv_width)
    low_rank_gradient = jnp.concatenate(
        [
            jnp.einsum(
                "trc,tkc->trk",
                gradient_per_tile[:, :, :kv_width],
                fac_b[:, :rank_one],
                preferred_element_type=jnp.float32,
            ),
            jnp.einsum(
                "trc,tkc->trk",
                gradient_per_tile[:, :, kv_width:],
                fac_b[:, rank_one:],
                preferred_element_type=jnp.float32,
            ),
        ],
        axis=2,
    ).astype(jnp.bfloat16)
    backward_pass = jnp.einsum("rc,ec->re", grad_rows, weight, preferred_element_type=jnp.float32)
    backward_adapter_term = jnp.einsum(
        "qdu,qyu->qdy", low_rank_gradient, factor_down, preferred_element_type=jnp.float32
    )
    token_gradient = (
        backward_pass
        + adapter_scale * backward_adapter_term.reshape(grouped_row_count, feature_shard)
    ).astype(jnp.bfloat16)
    tile_down_gradient = adapter_scale * jnp.einsum(
        "tre,trk->tek", token_tile_index, low_rank_gradient, preferred_element_type=jnp.float32
    )
    col_start = lax.axis_index("tp") * kv_dev
    key_cols = lax.dynamic_slice_in_dim(gradient_per_tile[:, :, :kv_width], col_start, kv_dev, 2)
    value_cols = lax.dynamic_slice_in_dim(gradient_per_tile[:, :, kv_width:], col_start, kv_dev, 2)
    tile_up_gradient = adapter_scale * jnp.concatenate(
        [
            jnp.einsum(
                "trk,trc->tkc",
                rank_act[:, :, :rank_one],
                key_cols,
                preferred_element_type=jnp.float32,
            ),
            jnp.einsum(
                "trk,trc->tkc",
                rank_act[:, :, rank_one:],
                value_cols,
                preferred_element_type=jnp.float32,
            ),
        ],
        axis=1,
    )
    size_a = feature_shard * rank_two
    flat_grads = jnp.concatenate(
        [tile_down_gradient.reshape(tile_count, -1), tile_up_gradient.reshape(tile_count, -1)],
        axis=1,
    )
    one_hot = (
        tile_index_list[:, None]
        == jnp.arange(adapt_local * lax.axis_size("blk"), dtype=jnp.int32)[None, :]
    ).astype(jnp.float32)
    summed = lax.psum_scatter(
        jnp.dot(
            one_hot.T,
            flat_grads,
            precision=lax.Precision.HIGHEST,
            preferred_element_type=jnp.float32,
        ),
        "blk",
        scatter_dimension=0,
        tiled=True,
    )
    grad_a = summed[:, :size_a].reshape(adapt_local, feature_shard, rank_two)
    grad_b = summed[:, size_a:].reshape(adapt_local, rank_two, kv_dev)
    return (key_value_output, token_gradient, grad_a, grad_b)


def solution(mesh):
    in_specs = (
        P("blk", "tp"),
        P("tp", None),
        P("blk", "tp", None),
        P("blk", None, None),
        P("blk", None),
        P(("blk", "tp"), None),
    )
    out_specs = (P(("blk", "tp"), None), P("blk", "tp"), P("blk", "tp", None), P("blk", None, "tp"))
    return jax.shard_map(
        on_device, mesh=mesh, in_specs=in_specs, out_specs=out_specs, check_vma=False
    )
```

profile of v0, /device:TPU:1, one launch (start us, length us, event | category | flops | bytes accessed | tf_op | source)
XLA Modules:
  0.0 530.9 jit_solution(16734941255564982452)
XLA Ops:
  7.2 0.7 all-gather.8.cloned.1.call-update
  8.0 0.7 all-gather.4.cloned.1.call-update
  8.7 0.7 all-gather.6.cloned.1.call-update
  9.5 4.8 fusion.45
  14.3 50.2 %all-gather.8.cloned.1.call-done = bf16[256,2048]{1,0:T(8,128)(2,1)} async-done(((bf16[32,2048]{1,0:T(8,128)(2,1)}), bf16[256,2048]{1,0:T(8,128)(2,1)}) %all-gather.8.cloned.1.call-update) | async-done | bytes 1048592 | tf_op jit(solution)/shard_map/all_gather | solution.py:76
  64.5 2.1 fusion.43
  66.6 65.2 %all-gather.4.cloned.1.call-done = bf16[32,1024,32]{1,2,0:T(8,128)(2,1)} async-done(((bf16[1,1024,32]{1,2,0:T(8,128)(2,1)}), bf16[32,1024,32]{1,2,0:T(8,128)(2,1)}) %all-gather.4.cloned.1.call-update) | async-done | bytes 2097168 | tf_op jit(solution)/shard_map/all_gather | solution.py:27
  131.7 7.8 %copy.28 = bf16[32,1024,32]{2,1,0:T(8,128)(2,1)} copy(bf16[32,1024,32]{1,2,0:T(8,128)(2,1)} %all-gather.4.cloned.1.call-done) | data formatting | bytes 4194304 | tf_op jit(solution)/shard_map/all_gather | solution.py:27
  139.5 10.5 %reshape.43 = bf16[32,32768]{1,0:T(8,128)(2,1)S(1)} reshape(bf16[32,1024,32]{2,1,0:T(8,128)(2,1)} %copy.28) | data formatting | bytes 4194304 | tf_op jit(solution)/shard_map/reshape | solution.py:36
  150.0 8.0 %dot_general.58 = bf16[1024,32,32]{1,0,2:T(8,128)(2,1)} reshape(bf16[32768,32]{0,1:T(8,128)(2,1)S(1)} %bitcast.50) | data formatting | bytes 4194304 | tf_op jit(solution)/shard_map/dot_general | solution.py:35
  158.1 7.5 %copy.29 = bf16[1024,32,32]{0,2,1:T(8,128)(2,1)S(1)} copy(bf16[1024,32,32]{1,0,2:T(8,128)(2,1)} %dot_general.58) | data formatting | bytes 4194304 | tf_op jit(solution)/shard_map/dot_general | solution.py:35
  165.6 0.5 convolution_convert_fusion
  166.3 34.4 %psum.7 = bf16[2,128,32]{1,2,0:T(8,128)(2,1)S(1)} all-reduce(f32[2,128,32]{1,2,0:T(8,128)S(1)} %convolution_bitcast_fusion), channel_id=1, replica_groups=mesh['blk'=32,'tp'=8] {'tp'}, use_global_device_ids=true, to_apply=%region_1.0 | all-reduce | flops 8192 | bytes 49152 | tf_op jit(solution)/shard_map/psum | solution.py:47
  200.7 1.0 fusion.16
  201.9 3.9 fusion.5
  206.6 0.3 copy.37
  207.0 0.6 reshape.48
  207.5 3.9 fusion.10
  211.4 0.6 copy-done.5
  212.1 0.6 dynamic-slice
  212.7 0.3 fusion.21
  213.0 0.3 fusion.24
  213.4 0.3 convolution_multiply_fusion
  213.9 1.7 copy-done.4
  215.6 0.4 copy-done.2
  215.9 2.1 fusion.3
  218.0 61.8 %reduce-scatter.2.cloned.1.call-done = f32[32,2048]{1,0:T(8,128)} async-done(((f32[256,2048]{1,0:T(8,128)}), f32[32,2048]{1,0:T(8,128)}) %reduce-scatter.2.cloned.1.call-update) | async-done | bytes 262160 | tf_op jit(solution)/shard_map/reduce_scatter | solution.py:48
  279.8 1.6 add_convert_fusion
  281.4 237.6 %all-reduce.3.cloned.1.call-done = f32[32,36864]{1,0:T(8,128)} async-done(((f32[32,36864]{1,0:T(8,128)}), f32[32,36864]{1,0:T(8,128)}) %all-reduce.3.cloned.1.call-update) | async-done | bytes 4718608
  519.0 2.1 dynamic-slice_reduce_fusion
  521.3 0.8 copy.38
  522.2 2.2 dynamic-slice.3
  (27 shorter events, 1.8 us)
Async XLA Ops:
  7.2 2.3 copy-start
  7.2 57.3 %all-gather.8.cloned.1.call-start = ((), (), s32[]{:S(2)}) async-start(), calls=%async_computation.4 | async-start | bytes 1179648 | tf_op jit(solution)/shard_map/all_gather | solution.py:76
  7.9 123.8 %all-gather.4.cloned.1.call-start = ((), (), s32[]{:S(2)}) async-start(), calls=%async_computation.2 | async-start | bytes 2162688 | tf_op jit(solution)/shard_map/all_gather | solution.py:27
  8.7 193.2 %all-gather.6.cloned.1.call-start = ((), (), s32[]{:S(2)}) async-start(), calls=%async_computation.3 | async-start | bytes 2162688 | tf_op jit(solution)/shard_map/all_gather | solution.py:28
  9.4 270.4 %reduce-scatter.2.cloned.1.call-start = ((), (), s32[]{:S(2)}) async-start(), calls=%async_computation.1 | async-start | bytes 2359296 | tf_op jit(solution)/shard_map/reduce_scatter | solution.py:48
  14.2 504.8 %all-reduce.3.cloned.1.call-start = ((), (), s32[]{:S(2)}) async-start(), calls=%async_computation.5 | async-start | bytes 9437184
  158.1 7.5 %copy-start.3 = (s32[2,1]{0,1:T(1,128)S(1)}, s32[2,1]{0,1:T(1,128)}, u32[]{:S(2)}) copy-start(s32[2,1]{0,1:T(1,128)} %param.10) | copy-start | bytes 28
  166.1 39.8 %copy-start.1 = (bf16[256,2048]{1,0:T(8,128)(2,1)S(1)}, bf16[256,2048]{1,0:T(8,128)(2,1)}, u32[]{:S(2)}) copy-start(bf16[256,2048]{1,0:T(8,128)(2,1)} %all-gather.8.cloned.1.call-done) | copy-start | bytes 3145732
  211.4 0.7 copy-start.5
  213.4 2.2 copy-start.4
  213.7 2.2 copy-start.2
Sparse Core Ops, SparseCore 0:
  10.7 53.7 all-gather.7
  66.3 65.3 all-gather.3
  133.6 64.5 all-gather.5
  202.0 77.7 reduce-scatter.1
  282.3 236.6 all-reduce.2
where the time goes:
time: 532 us; the launch traced here: 531 us
  waiting for transfers between devices  417 us (78%)
  local copies, waits for them, and re-layouts  45.6 us (9%)
  blocking collectives  34.4 us (6%)
  matrix products  18.2 us (3%)
  between operations  13.9 us (3%)
    unnamed x6, waiting for transfers between devices  240 us
    all_gather x1, waiting for transfers between devices, on_device(): lax.all_gather(bank_a, 'blk', axis=0, tiled=True)  65.2 us
    reduce_scatter x1, waiting for transfers between devices, on_device(): lax.psum_scatter(jnp.dot(tokens, weight, preferred_element_type=jnp.float...  61.8 us
    all_gather x1, waiting for transfers between devices, on_device(): grad_rows = lax.all_gather(grad_out, 'tp', axis=0, tiled=True)  50.2 us
    psum x1, blocking collectives, on_device(): rank_act = lax.psum(rank_part, 'tp').astype(jnp.bfloat16)  34.4 us
    dot_general x2, local copies, waits for them, and re-layouts, on_device(): jnp.dot(one_hot, pieces[0].reshape(piece_rows, -1), preferred_element_typ...  15.6 us
  transfers between devices with their start and end apart: 5, of which 4 were waited for; matrix products, arithmetic and copies ran while one was open for 11% of the time, Pallas kernels for 0%

commit v1 on v0

--- a/solution.py
+++ b/solution.py
@@ -1,9 +1,22 @@
+import functools
 import jax
 import jax.numpy as jnp
 from jax import lax
 from jax.sharding import PartitionSpec as P
 
 adapter_scale = 0.5
+
+
+def search_the_scenes(inputs, peer_axis):
+    return jnp.concatenate(
+        lax.all_to_all(
+            jnp.stack([inputs] * lax.axis_size(peer_axis)), peer_axis, concat_axis=0, split_axis=0
+        ),
+        axis=0,
+    )
+
+
+_return_all_matrix = functools.partial(search_the_scenes, peer_axis="blk")
 
 
 def on_device(tokens, weight, bank_a, bank_b, tile_map, grad_out):
@@ -24,7 +37,7 @@
         jnp.zeros((tile_count, rank_two, kv_width), jnp.bfloat16),
     )
     whole_a, whole_b = (
-        lax.all_gather(bank_a, "blk", axis=0, tiled=True),
+        _return_all_matrix(bank_a),
         lax.all_gather(bank_b, "blk", axis=0, tiled=True),
     )
     pieces = (whole_a, whole_b)

time: 532 us -> 470 us (0.88)
  waiting for transfers between devices: 417 us -> 345 us
  starting transfers between devices: 0.19 us -> 11.2 us
    all_gather x1 -> x0, waiting for transfers between devices: 65.2 us -> none  [on_device(): lax.all_gather(bank_a, 'blk', axis=0, tiled=True)]
    another operation x0 -> x2, local copies, waits for them, and re-layouts: none -> 13 us  [the longest x1 10.5 us: on_device(): pieces[0].reshape(piece_rows, -1)]
    all_to_all x0 -> x1, starting transfers between devices: none -> 11.1 us  [search_the_scenes(): lax.all_to_all(jnp.stack([inputs] * lax.axis_size(peer_axis)), peer_axis,...]
    reshape x1 -> x0, local copies, waits for them, and re-layouts: 10.5 us -> none  [on_device(): pieces[0].reshape(piece_rows, -1)]
    all_gather x1 -> x0, local copies, waits for them, and re-layouts: 7.76 us -> none  [on_device(): lax.all_gather(bank_a, 'blk', axis=0, tiled=True)]
    all_to_all x0 -> x1, local copies, waits for them, and re-layouts: none -> 5.97 us  [search_the_scenes(): lax.all_to_all(jnp.stack([inputs] * lax.axis_size(peer_axis)), peer_axis,...]
    all_gather x1, waiting for transfers between devices: 50.2 us -> 44.2 us  [on_device(): grad_rows = lax.all_gather(grad_out, 'tp', axis=0, tiled=True)]
    unnamed x6 -> x5, waiting for transfers between devices: 240 us -> 239 us
  transfers between devices with their start and end apart: 5 -> 5, of which waited for: 4 -> 3; matrix products, arithmetic and copies ran while one was open for 11% -> 12% of each run, Pallas kernels for 0% -> 0%
where the time goes in v1:
time: 470 us; the launch traced here: 469 us
  waiting for transfers between devices  345 us (73%)
  local copies, waits for them, and re-layouts  46.4 us (10%)
  blocking collectives  32.9 us (7%)
  matrix products  18.2 us (4%)
  between operations  13.9 us (3%)
  starting transfers between devices  11.2 us (2%)
    unnamed x5, waiting for transfers between devices  239 us
    reduce_scatter x1, waiting for transfers between devices, on_device(): lax.psum_scatter(jnp.dot(tokens, weight, preferred_element_type=jnp.float...  61.5 us
    all_gather x1, waiting for transfers between devices, on_device(): grad_rows = lax.all_gather(grad_out, 'tp', axis=0, tiled=True)  44.2 us
    psum x1, blocking collectives, on_device(): rank_act = lax.psum(rank_part, 'tp').astype(jnp.bfloat16)  32.9 us
    dot_general x2, local copies, waits for them, and re-layouts, on_device(): jnp.dot(one_hot, pieces[0].reshape(piece_rows, -1), preferred_element_typ...  15.6 us
    all_to_all x1, starting transfers between devices, search_the_scenes(): lax.all_to_all(jnp.stack([inputs] * lax.axis_size(peer_axis)), peer_axis,...  11.1 us
    another operation x1, local copies, waits for them, and re-layouts, on_device(): pieces[0].reshape(piece_rows, -1)  10.5 us
  transfers between devices with their start and end apart: 5, of which 3 were waited for; matrix products, arithmetic and copies ran while one was open for 12% of the time, Pallas kernels for 0%

profile of v1, /device:TPU:1, one launch (start us, length us, event | category | flops | bytes accessed | tf_op | source)
XLA Modules:
  0.0 469.4 jit_solution(12672360994793539924)
XLA Ops:
  7.2 0.7 all-gather.5.cloned.1.call-update
  8.0 0.7 all-gather.3.cloned.1.call-update
  8.7 2.4 stack.2
  11.1 11.1 %all-to-all-start = ((bf16[32,1,1024,32]{2,3,1,0:T(8,128)(2,1)}), bf16[32,1,1024,32]{2,3,1,0:T(8,128)(2,1)S(1)}, u32[]{:S(2)}, u32[]{:S(2)}) async-start(bf16[32,1,1024,32]{2,3,1,0:T(8,128)(2,1)} %stack.2), calls=%async_computation.1 | async-start | bytes 4194304 | tf_op jit(solution)/shard_map/all_to_all | solution.py:12
  22.2 4.8 %fusion.45 = f32[256,2048]{1,0:T(8,128)} fusion(bf16[256,1024]{1,0:T(8,128)(2,1)S(1)} %copy-done, bf16[1024,2048]{1,0:T(8,128)(2,1)} %param.7), kind=kOutput, calls=%fused_computation.58 | convolution fusion | flops 1073741824 | bytes 6815744 | tf_op jit(solution)/shard_map/dot_general | solution.py:62
  27.1 44.2 %all-gather.5.cloned.1.call-done = bf16[256,2048]{1,0:T(8,128)(2,1)} async-done(((bf16[32,2048]{1,0:T(8,128)(2,1)}), bf16[256,2048]{1,0:T(8,128)(2,1)}) %all-gather.5.cloned.1.call-update) | async-done | bytes 1048592 | tf_op jit(solution)/shard_map/all_gather | solution.py:89
  71.3 2.1 fusion.43
  73.4 6.0 %copy.29 = bf16[32,1,1024,32]{3,2,0,1:T(8,128)(2,1)} copy(bf16[32,1,1024,32]{2,3,1,0:T(8,128)(2,1)S(1)} %all-to-all-done) | data formatting | bytes 4194304 | tf_op jit(solution)/shard_map/all_to_all | solution.py:12
  79.3 10.5 %reshape_reshape.3 = bf16[32,32768]{1,0:T(8,128)(2,1)S(1)} reshape(bf16[32,1,1024,32]{3,2,0,1:T(8,128)(2,1)} %copy.29) | data formatting | bytes 4194304 | tf_op jit(solution)/shard_map/reshape;reshape | solution.py:49
  89.9 8.0 %dot_general.58 = bf16[1024,32,32]{1,0,2:T(8,128)(2,1)} reshape(bf16[32768,32]{0,1:T(8,128)(2,1)S(1)} %bitcast.55) | data formatting | bytes 4194304 | tf_op jit(solution)/shard_map/dot_general | solution.py:48
  97.9 7.5 %copy.30 = bf16[1024,32,32]{0,2,1:T(8,128)(2,1)S(1)} copy(bf16[1024,32,32]{1,0,2:T(8,128)(2,1)} %dot_general.58) | data formatting | bytes 4194304 | tf_op jit(solution)/shard_map/dot_general | solution.py:48
  105.5 0.5 convolution_convert_fusion
  106.2 32.9 %psum.7 = bf16[2,128,32]{1,2,0:T(8,128)(2,1)S(1)} all-reduce(f32[2,128,32]{1,2,0:T(8,128)S(1)} %convolution_bitcast_fusion), channel_id=1, replica_groups=mesh['blk'=32,'tp'=8] {'tp'}, use_global_device_ids=true, to_apply=%region_1.0 | all-reduce | flops 8192 | bytes 49152 | tf_op jit(solution)/shard_map/psum | solution.py:60
  139.1 1.0 fusion.16
  140.3 3.9 fusion.5
  145.0 0.3 copy.38
  145.4 0.6 reshape.47
  145.9 3.9 fusion.10
  149.9 0.6 copy-done.5
  150.5 0.6 dynamic-slice
  151.1 0.3 fusion.21
  151.4 0.3 fusion.24
  151.8 0.3 convolution_multiply_fusion
  152.3 1.7 copy-done.4
  154.0 0.4 copy-done.2
  154.4 2.1 fusion.3
  156.4 61.5 %reduce-scatter.2.cloned.1.call-done = f32[32,2048]{1,0:T(8,128)} async-done(((f32[256,2048]{1,0:T(8,128)}), f32[32,2048]{1,0:T(8,128)}) %reduce-scatter.2.cloned.1.call-update) | async-done | bytes 262160 | tf_op jit(solution)/shard_map/reduce_scatter | solution.py:61
  217.9 1.6 add_convert_fusion
  219.6 237.8 %all-reduce.3.cloned.1.call-done = f32[32,36864]{1,0:T(8,128)} async-done(((f32[32,36864]{1,0:T(8,128)}), f32[32,36864]{1,0:T(8,128)}) %all-reduce.3.cloned.1.call-update) | async-done | bytes 4718608
  457.4 2.2 dynamic-slice_reduce_fusion
  459.8 0.8 copy.39
  460.6 2.2 dynamic-slice.3
  (27 shorter events, 1.8 us)
Async XLA Ops:
  7.2 15.0 %copy-start = (bf16[256,1024]{1,0:T(8,128)(2,1)S(1)}, bf16[256,1024]{1,0:T(8,128)(2,1)}, u32[]{:S(2)}) copy-start(bf16[256,1024]{1,0:T(8,128)(2,1)} %param.6) | copy-start | bytes 1572868
  7.2 64.1 %all-gather.5.cloned.1.call-start = ((), (), s32[]{:S(2)}) async-start(), calls=%async_computation.4 | async-start | bytes 1179648 | tf_op jit(solution)/shard_map/all_gather | solution.py:89
  7.9 132.3 %all-gather.3.cloned.1.call-start = ((), (), s32[]{:S(2)}) async-start(), calls=%async_computation.3 | async-start | bytes 2162688 | tf_op jit(solution)/shard_map/all_gather | solution.py:41
  11.1 62.3 %all-to-all-start = ((bf16[32,1,1024,32]{2,3,1,0:T(8,128)(2,1)}), bf16[32,1,1024,32]{2,3,1,0:T(8,128)(2,1)S(1)}, u32[]{:S(2)}, u32[]{:S(2)}) async-start(bf16[32,1,1024,32]{2,3,1,0:T(8,128)(2,1)} %stack.2), calls=%async_computation.1 | async-start | bytes 4194304 | tf_op jit(solution)/shard_map/all_to_all | solution.py:12
  22.2 195.8 %reduce-scatter.2.cloned.1.call-start = ((), (), s32[]{:S(2)}) async-start(), calls=%async_computation.2 | async-start | bytes 2359296 | tf_op jit(solution)/shard_map/reduce_scatter | solution.py:61
  27.0 430.4 %all-reduce.3.cloned.1.call-start = ((), (), s32[]{:S(2)}) async-start(), calls=%async_computation.5 | async-start | bytes 9437184
  97.9 7.5 %copy-start.3 = (s32[2,1]{0,1:T(1,128)S(1)}, s32[2,1]{0,1:T(1,128)}, u32[]{:S(2)}) copy-start(s32[2,1]{0,1:T(1,128)} %param.10) | copy-start | bytes 28
  105.9 38.4 %copy-start.1 = (bf16[256,2048]{1,0:T(8,128)(2,1)S(1)}, bf16[256,2048]{1,0:T(8,128)(2,1)}, u32[]{:S(2)}) copy-start(bf16[256,2048]{1,0:T(8,128)(2,1)} %all-gather.5.cloned.1.call-done) | copy-start | bytes 3145732
  149.8 0.7 copy-start.5
  151.8 2.2 copy-start.4
  152.1 2.2 copy-start.2
Sparse Core Ops, SparseCore 0:
  10.7 60.5 all-gather.4
  73.1 62.7 all-gather.2
  139.9 77.9 reduce-scatter.1
  220.4 236.8 all-reduce.2
